TPU v7x, 128 devices: a whole 4x4x4 slice. The times are simulated.
128 devices in a mesh: dp: 4 (over z), fsdp: 32 (over y, x, core).
Axes of the slice: x: 4, y: 4, z: 4, core: 2. Of those that a mesh axis runs over, the one named last changes fastest.
Arguments:
- logged: bfloat16 [2048, 8192], P('dp', 'fsdp'), may hold values from -6 to 6
- pairs: int32 [512, 2], P('dp'), may hold values from 0 to 511
- clicks: int32 [512], P('dp'), may hold values 0 or 1
- query_pairs: int32 [32, 2], P('dp'), may hold values from 0 to 511
- query_clicks: int32 [32], P('dp'), may hold values 0 or 1
- first_weight: bfloat16 [8192, 8192], P(None, 'fsdp'), may hold values from -0.0625 to 0.0625
- second_weight: bfloat16 [8192, 8192], P(None, 'fsdp'), may hold values from -0.0625 to 0.0625
- head_weight: float32 [8192], P('fsdp'), may hold values from -0.0625 to 0.0625
Outputs:
- solution: float32 [8192, 8192], P('dp', 'fsdp')
- influence: float32 [512], P('dp')
Inputs may be any that keep to these rules, and one draw needn't show every extreme that they name: Each block of 128 pairs indexes rows within the matching block of 512 logged rows. `query_pairs`: each block of 8 query pairs indexes rows within the matching block of 512 logged rows.
All inputs are finite; a program needn't handle non-finite values. No bound on the sum of `clicks` or of `query_clicks` on one device may be relied on, other than what follows from the above.
Results may differ from a plain program's by a relative error of at most 0.035.
Values may be sent and summed in bfloat16 or wider, within the bound.
A program may use at most 128 MiB of HBM per device.

v0:
```python
import jax
import jax.numpy as jnp
from jax import lax
from jax.sharding import PartitionSpec as P

DAMPING = 0.01


def pair_terms(first_score, second_score, outcome):
    signed = 2.0 * outcome.astype(jnp.float32) - 1.0
    margin = first_score - second_score
    slope_term = -signed * jax.nn.sigmoid(-signed * margin)
    curve_term = jax.nn.sigmoid(signed * margin) * jax.nn.sigmoid(-signed * margin)
    return (slope_term, curve_term)


def solver_total(value):
    return lax.psum(value, ("dp", "fsdp"))


def contract_rows(left, right):
    return lax.dot_general(
        left, right, (((0,), (0,)), ((), ())), preferred_element_type=jnp.float32
    )


def local(
    logged, pairs, clicks, query_pairs, query_clicks, first_weight, second_weight, head_weight
):
    npairs = pairs.shape[0]
    nqueries = query_pairs.shape[0]
    count = 2 * npairs
    row_ids = jnp.concatenate([pairs[:, 0], pairs[:, 1], query_pairs[:, 0], query_pairs[:, 1]])
    local_rows = jnp.take(logged, row_ids, axis=0)
    feats = lax.all_gather(local_rows, "fsdp", axis=1, tiled=True)
    hidden = jnp.tanh(jnp.dot(feats, first_weight, preferred_element_type=jnp.float32)).astype(
        jnp.bfloat16
    )
    second_pre = jnp.dot(
        lax.all_gather(hidden, "fsdp", axis=1, tiled=True),
        second_weight,
        preferred_element_type=jnp.float32,
    )
    output_act = jnp.tanh(second_pre)
    scores_all = lax.psum(jnp.sum(output_act * head_weight, axis=1), "fsdp")
    coef = (head_weight * (1.0 - output_act * output_act)).astype(jnp.bfloat16)
    back_term = lax.dot_general(
        coef, second_weight, (((1,), (1,)), ((), ())), preferred_element_type=jnp.float32
    )
    back = lax.psum_scatter(
        back_term.astype(jnp.bfloat16), "fsdp", scatter_dimension=1, tiled=True
    ).astype(jnp.float32)
    hidden_float = hidden.astype(jnp.float32)
    mixing = (1.0 - hidden_float * hidden_float) * back
    slope_train, curve_train = pair_terms(scores_all[:npairs], scores_all[npairs:count], clicks)
    slope_query = pair_terms(
        scores_all[count : count + nqueries], scores_all[count + nqueries :], query_clicks
    )[0]
    query_err = jnp.concatenate([slope_query, -slope_query])
    query_rows = (query_err[:, None] * mixing[count:]).astype(jnp.bfloat16)
    grad_local = contract_rows(feats[count:], query_rows)
    gradient = lax.psum_scatter(
        grad_local.astype(jnp.bfloat16), "dp", scatter_dimension=0, tiled=True
    ).astype(jnp.float32)
    train_feats = feats[:count]
    train_mix = mixing[:count]

    def apply_curvature(direction):
        packed = direction.astype(jnp.bfloat16)
        gathered = lax.all_gather(packed, "dp", axis=0, tiled=True)
        project = jnp.dot(train_feats, gathered, preferred_element_type=jnp.float32)
        response = lax.psum(jnp.sum(train_mix * project, axis=1), "fsdp")
        rdiff = response[:npairs] - response[npairs:]
        resp_err = jnp.concatenate([curve_train * rdiff, -curve_train * rdiff])
        resp_rows = (resp_err[:, None] * train_mix).astype(jnp.bfloat16)
        term = contract_rows(train_feats, resp_rows)
        return (packed, gathered, term, rdiff)

    norm_first = solver_total(jnp.sum(gradient * gradient))
    packed_first, gathered_first, local_first, rdiff_first = apply_curvature(gradient)
    product_first = lax.psum_scatter(
        local_first.astype(jnp.bfloat16), "dp", scatter_dimension=0, tiled=True
    ).astype(jnp.float32)
    curv_first = (
        solver_total(jnp.sum(packed_first.astype(jnp.float32) * product_first))
        + DAMPING * norm_first
    )
    alpha_first = norm_first / curv_first
    residual_next = gradient - alpha_first * (product_first + DAMPING * gradient)
    norm_next = solver_total(jnp.sum(residual_next * residual_next))
    direction_next = residual_next + norm_next / norm_first * gradient
    packed_next, gathered_next, local_next, rdiff_next = apply_curvature(direction_next)
    damped_part = DAMPING * jnp.sum(direction_next * direction_next)
    product_next = lax.psum_scatter(
        local_next.astype(jnp.bfloat16), "dp", scatter_dimension=0, tiled=True
    ).astype(jnp.float32)
    inner_part = jnp.sum(packed_next.astype(jnp.float32) * product_next) + damped_part
    curv_next = solver_total(inner_part)
    alpha_next = norm_next / curv_next
    solution = alpha_first * gradient + alpha_next * direction_next
    influence = -slope_train * (alpha_first * rdiff_first + alpha_next * rdiff_next)
    return (solution, influence)


def solution(mesh):
    placed = (
        P("dp", "fsdp"),
        P("dp", None),
        P("dp"),
        P("dp", None),
        P("dp"),
        P(None, "fsdp"),
        P(None, "fsdp"),
        P("fsdp"),
    )
    return jax.shard_map(
        local, mesh=mesh, in_specs=placed, out_specs=(P("dp", "fsdp"), P("dp")), check_vma=False
    )
```

profile of v0, /device:TPU:1, one launch (start us, length us, event | category | flops | bytes accessed | tf_op | source)
XLA Modules:
  0.0 815.9 jit_solution(4647815058639752397)
XLA Ops:
  7.2 0.0 all-gather.5.cloned.1.call-start
  7.2 0.8 slice_bitcast_fusion.3
  8.0 0.8 slice_bitcast_fusion.1
  8.7 0.1 fusion.33
  8.8 2.0 gather_fusion
  10.8 0.1 compare_and_fusion
  10.9 0.8 broadcast_select_fusion
  11.7 0.0 all-gather.5.cloned.1.call-update
  11.7 0.0 all-gather.7.cloned.1.call-start
  11.8 53.5 %all-gather.5.cloned.1.call-done = bf16[272,8192]{1,0:T(8,128)(2,1)} async-done(((bf16[272,256]{1,0:T(8,128)(2,1)}), bf16[272,8192]{1,0:T(8,128)(2,1)}) %all-gather.5.cloned.1.call-update) | async-done | bytes 4456464 | tf_op jit(solution)/shard_map/all_gather | solution.py:35
  65.2 5.5 fusion.17
  70.8 0.0 all-gather.7.cloned.1.call-update
  70.8 0.0 reduce-scatter.5.cloned.1.call-start
  70.8 49.4 %all-gather.7.cloned.1.call-done = bf16[272,8192]{1,0:T(8,128)(2,1)} async-done(((bf16[272,256]{1,0:T(8,128)(2,1)}), bf16[272,8192]{1,0:T(8,128)(2,1)}) %all-gather.7.cloned.1.call-update) | async-done | bytes 4456464 | tf_op jit(solution)/shard_map/all_gather | solution.py:40
  120.2 5.1 multiply_reduce_fusion.3
  125.4 3.5 convolution_convert_fusion
  128.8 0.0 reduce-scatter.5.cloned.1.call-update
  128.8 0.0 reduce-scatter.7.cloned.1.call-start
  128.9 62.7 %psum.49 = f32[272]{0:T(512)S(1)} all-reduce(f32[272]{0:T(512)S(1)} %get-tuple-element.23), channel_id=1, replica_groups=mesh['dp'=4,'fsdp'=32] {'fsdp'}, use_global_device_ids=true, to_apply=%region_1.2 | all-reduce | flops 272 | bytes 2176 | tf_op jit(solution)/shard_map/psum | solution.py:45
  191.6 0.1 fusion.37
  191.7 0.1 pad_maximum_fusion.2
  191.7 18.3 %reduce-scatter.5.cloned.1.call-done = bf16[272,256]{1,0:T(8,128)(2,1)} async-done(((bf16[272,8192]{1,0:T(8,128)(2,1)}), bf16[272,256]{1,0:T(8,128)(2,1)}) %reduce-scatter.5.cloned.1.call-update) | async-done | bytes 139280 | tf_op jit(solution)/shard_map/reduce_scatter | solution.py:50
  210.1 1.0 convert_multiply_fusion.5
  211.0 4.2 convolution_convert_fusion.3
  215.3 0.0 all-gather.9.cloned.1.call-start
  215.3 48.5 %reduce-scatter.7.cloned.1.call-done = bf16[2048,256]{1,0:T(8,128)(2,1)} async-done(((bf16[8192,256]{1,0:T(8,128)(2,1)}), bf16[2048,256]{1,0:T(8,128)(2,1)}) %reduce-scatter.7.cloned.1.call-update) | async-done | bytes 1048592 | tf_op jit(solution)/shard_map/reduce_scatter | solution.py:62
  263.9 0.0 reduce-scatter.9.cloned.1.call-start
  263.9 49.5 %all-gather.9.cloned.1.call-done = bf16[8192,256]{1,0:T(8,128)(2,1)} async-done(((bf16[2048,256]{1,0:T(8,128)(2,1)}), bf16[8192,256]{1,0:T(8,128)(2,1)}) %all-gather.9.cloned.1.call-update) | async-done | bytes 4194320 | tf_op jit(solution)/shard_map/all_gather | solution.py:70
  313.4 4.8 fusion.22
  318.2 62.7 %psum.51 = f32[256]{0:T(256)S(1)} all-reduce(f32[256]{0:T(256)S(1)} %fusion.22), channel_id=1, replica_groups=mesh['dp'=4,'fsdp'=32] {'fsdp'}, use_global_device_ids=true, to_apply=%region_7.8 | all-reduce | flops 256 | bytes 2048 | tf_op jit(solution)/shard_map/psum | solution.py:72
  380.9 5.5 convolution_convert_fusion.2
  386.5 0.0 all-gather.11.cloned.1.call-start
  386.5 46.8 %reduce-scatter.9.cloned.1.call-done = bf16[2048,256]{1,0:T(8,128)(2,1)} async-done(((bf16[8192,256]{1,0:T(8,128)(2,1)}), bf16[2048,256]{1,0:T(8,128)(2,1)}) %reduce-scatter.9.cloned.1.call-update) | async-done | bytes 1048592 | tf_op jit(solution)/shard_map/reduce_scatter | solution.py:81
  433.3 2.5 fusion.8
  435.8 64.6 %all-reduce = (f32[]{:T(128)}, f32[]{:T(128)}) all-reduce(f32[]{:T(128)} %get-tuple-element.3, f32[]{:T(128)} %get-tuple-element.2), channel_id=1, replica_groups=mesh['dp'=4,'fsdp'=32] {'dp','fsdp'}, use_global_device_ids=true, to_apply=%region_5.6 | all-reduce | flops 2 | bytes 16 | tf_op jit(solution)/shard_map/psum | solution.py:18
  502.3 2.4 multiply_reduce_fusion.2
  504.7 64.3 %psum.53 = f32[]{:T(128)} all-reduce(f32[]{:T(128)} %multiply_reduce_fusion.2), channel_id=1, replica_groups=mesh['dp'=4,'fsdp'=32] {'dp','fsdp'}, use_global_device_ids=true, to_apply=%region_12.13 | all-reduce | flops 1 | bytes 8 | tf_op jit(solution)/shard_map/psum | solution.py:18
  570.4 2.3 multiply_reduce_fusion
  572.7 0.0 reduce-scatter.11.cloned.1.call-start
  572.7 45.0 %all-gather.11.cloned.1.call-done = bf16[8192,256]{1,0:T(8,128)(2,1)} async-done(((bf16[2048,256]{1,0:T(8,128)(2,1)}), bf16[8192,256]{1,0:T(8,128)(2,1)}) %all-gather.11.cloned.1.call-update) | async-done | bytes 4194320 | tf_op jit(solution)/shard_map/all_gather | solution.py:70
  617.7 4.8 fusion.19
  622.5 62.7 %psum.54 = f32[256]{0:T(256)S(1)} all-reduce(f32[256]{0:T(256)S(1)} %fusion.19), channel_id=1, replica_groups=mesh['dp'=4,'fsdp'=32] {'fsdp'}, use_global_device_ids=true, to_apply=%region_14.15 | all-reduce | flops 256 | bytes 2048 | tf_op jit(solution)/shard_map/psum | solution.py:72
  685.2 5.5 convolution_convert_fusion.1
  691.5 46.1 %reduce-scatter.11.cloned.1.call-done = bf16[2048,256]{1,0:T(8,128)(2,1)} async-done(((bf16[8192,256]{1,0:T(8,128)(2,1)}), bf16[2048,256]{1,0:T(8,128)(2,1)}) %reduce-scatter.11.cloned.1.call-update) | async-done | bytes 1048592 | tf_op jit(solution)/shard_map/reduce_scatter | solution.py:94
  737.6 2.4 multiply_reduce_fusion.1
  740.6 64.5 %psum.55 = f32[]{:T(128)} all-reduce(f32[]{:T(128)S(6)} %add.83), channel_id=1, replica_groups=mesh['dp'=4,'fsdp'=32] {'dp','fsdp'}, use_global_device_ids=true, to_apply=%region_18.19 | all-reduce | flops 1 | bytes 8 | tf_op jit(solution)/shard_map/psum | solution.py:18
  806.5 0.5 add_multiply_fusion
  807.0 2.1 fusion.9
  (29 shorter events, 0.2 us)
Async XLA Ops:
  7.2 1.7 copy-start
  7.2 58.0 %all-gather.5.cloned.1.call-start = ((), (), s32[]{:S(2)}) async-start(), calls=%async_computation.4 | async-start | bytes 4595712 | tf_op jit(solution)/shard_map/all_gather | solution.py:35
  11.7 108.5 %copy-start.6 = (f32[256]{0:T(256)S(1)}, f32[256]{0:T(256)}, u32[]{:S(2)}) copy-start(f32[256]{0:T(256)} %param.15) | copy-start | bytes 3076
  11.7 108.5 %all-gather.7.cloned.1.call-start = ((), (), s32[]{:S(2)}) async-start(), calls=%async_computation.5 | async-start | bytes 4595712 | tf_op jit(solution)/shard_map/all_gather | solution.py:40
  70.8 139.3 %reduce-scatter.5.cloned.1.call-start = ((), (), s32[]{:S(2)}) async-start(), calls=%async_computation.6 | async-start | bytes 4595712 | tf_op jit(solution)/shard_map/reduce_scatter | solution.py:50
  120.2 5.1 copy-start.4
  128.8 62.8 %copy-start.8 = (s32[8]{0:T(128)S(1)}, s32[8]{0:T(128)}, u32[]{:S(2)}) copy-start(s32[8]{0:T(128)} %param.12) | copy-start | bytes 100
  128.8 81.3 %copy-start.5 = (bf16[272,256]{1,0:T(8,128)(2,1)S(1)}, bf16[272,256]{1,0:T(8,128)(2,1)}, u32[]{:S(2)}) copy-start(bf16[272,256]{1,0:T(8,128)(2,1)} %fusion.17) | copy-start | bytes 417796
  128.8 135.0 %reduce-scatter.7.cloned.1.call-start = ((), (), s32[]{:S(2)}) async-start(), calls=%async_computation.7 | async-start | bytes 5242880 | tf_op jit(solution)/shard_map/reduce_scatter | solution.py:62
  215.3 98.1 %all-gather.9.cloned.1.call-start = ((), (), s32[]{:S(2)}) async-start(), calls=%async_computation.8 | async-start | bytes 5242880 | tf_op jit(solution)/shard_map/all_gather | solution.py:70
  263.9 117.0 %copy-start.7 = (s32[128]{0:T(128)S(1)}, s32[128]{0:T(128)}, u32[]{:S(2)}) copy-start(s32[128]{0:T(128)} %param.10) | copy-start | bytes 1540
  263.9 169.4 %reduce-scatter.9.cloned.1.call-start = ((), (), s32[]{:S(2)}) async-start(), calls=%async_computation.9 | async-start | bytes 5242880 | tf_op jit(solution)/shard_map/reduce_scatter | solution.py:81
  386.4 46.9 %copy-start.1 = (bf16[2048,256]{1,0:T(8,128)(2,1)S(1)}, bf16[2048,256]{1,0:T(8,128)(2,1)}, u32[]{:S(2)}) copy-start(bf16[2048,256]{1,0:T(8,128)(2,1)} %reduce-scatter.7.cloned.1.call-done) | copy-start | bytes 3145732
  386.5 231.2 %all-gather.11.cloned.1.call-start = ((), (), s32[]{:S(2)}) async-start(), calls=%async_computation.10 | async-start | bytes 5242880 | tf_op jit(solution)/shard_map/all_gather | solution.py:70
  433.3 137.1 %copy-start.2 = (bf16[2048,256]{1,0:T(8,128)(2,1)S(1)}, bf16[2048,256]{1,0:T(8,128)(2,1)}, u32[]{:S(2)}) copy-start(bf16[2048,256]{1,0:T(8,128)(2,1)} %reduce-scatter.9.cloned.1.call-done) | copy-start | bytes 3145732
  572.7 164.9 %reduce-scatter.11.cloned.1.call-start = ((), (), s32[]{:S(2)}) async-start(), calls=%async_computation.11 | async-start | bytes 5242880 | tf_op jit(solution)/shard_map/reduce_scatter | solution.py:94
  690.7 46.9 %copy-start.3 = (bf16[2048,256]{1,0:T(8,128)(2,1)S(1)}, bf16[2048,256]{1,0:T(8,128)(2,1)}, u32[]{:S(2)}) copy-start(bf16[2048,256]{1,0:T(8,128)(2,1)} %get-tuple-element.12) | copy-start | bytes 3145732
Sparse Core Ops, SparseCore 0:
  11.8 53.3 all-gather.4
  70.9 49.2 all-gather.6
  129.0 81.0 reduce-scatter.4
  215.4 48.3 reduce-scatter.6
  265.4 47.9 all-gather.8
  386.6 46.6 reduce-scatter.8
  572.8 44.8 all-gather.10
  690.9 46.6 reduce-scatter.10
where the time goes:
time: 817 us; the launch traced here: 816 us
  blocking collectives  381 us (47%)
  waiting for transfers between devices  357 us (44%)
  matrix products  38.9 us (5%)
  between operations  20.2 us (2%)
  other arithmetic  14.2 us (2%)
    psum x3, blocking collectives, solver_total(): return lax.psum(value, ('dp', 'fsdp'))  193 us
    psum x2, blocking collectives, apply_curvature(): response = lax.psum(jnp.sum(train_mix * project, axis=1), 'fsdp')  125 us
    all_gather x2, waiting for transfers between devices, apply_curvature(): gathered = lax.all_gather(packed, 'dp', axis=0, tiled=True)  94.4 us
    psum x1, blocking collectives, local(): scores_all = lax.psum(jnp.sum(output_act * head_weight, axis=1), 'fsdp')  62.7 us
    all_gather x1, waiting for transfers between devices, local(): feats = lax.all_gather(local_rows, 'fsdp', axis=1, tiled=True)  53.5 us
    all_gather x1, waiting for transfers between devices, local(): lax.all_gather(hidden, 'fsdp', axis=1, tiled=True)  49.4 us
    reduce_scatter x1, waiting for transfers between devices, local(): lax.psum_scatter(grad_local.astype(jnp.bfloat16), 'dp', scatter_dimension...  48.5 us
    reduce_scatter x1, waiting for transfers between devices, local(): lax.psum_scatter(local_first.astype(jnp.bfloat16), 'dp', scatter_dimensio...  46.8 us
  transfers between devices with their start and end apart: 8, of which 8 were waited for; matrix products, arithmetic and copies ran while one was open for 0% of the time, Pallas kernels for 0%

commit v1 on v0

--- a/solution.py
+++ b/solution.py
@@ -4,6 +4,19 @@
 from jax.sharding import PartitionSpec as P
 
 DAMPING = 0.01
+
+
+def ring_gather(value, axis, dim):
+    ways = lax.axis_size(axis)
+    up = [(d, (d + 1) % ways) for d in range(ways)]
+    down = [(d, (d - 1) % ways) for d in range(ways)]
+    earlier, later = ([value], [value])
+    for _ in range(ways // 2):
+        earlier.append(lax.ppermute(earlier[-1], axis, up))
+    for _ in range((ways - 1) // 2):
+        later.append(lax.ppermute(later[-1], axis, down))
+    line = jnp.concatenate([*earlier[::-1], *later[1:]], axis=dim)
+    return jnp.roll(line, (lax.axis_index(axis) - ways // 2) * value.shape[dim], axis=dim)
 
 
 def pair_terms(first_score, second_score, outcome):
@@ -67,7 +80,7 @@
 
     def apply_curvature(direction):
         packed = direction.astype(jnp.bfloat16)
-        gathered = lax.all_gather(packed, "dp", axis=0, tiled=True)
+        gathered = ring_gather(packed, "dp", 0)
         project = jnp.dot(train_feats, gathered, preferred_element_type=jnp.float32)
         response = lax.psum(jnp.sum(train_mix * project, axis=1), "fsdp")
         rdiff = response[:npairs] - response[npairs:]

time: 817 us -> 871 us (1.066)
  matrix products: 38.9 us -> 88.7 us
  waiting for transfers between devices: 357 us -> 347 us
    all_gather x2 -> x0, waiting for transfers between devices: 94.4 us -> none  [apply_curvature(): gathered = lax.all_gather(packed, 'dp', axis=0, tiled=True)]
    ppermute x0 -> x6, waiting for transfers between devices: none -> 93.7 us  [the longest x4 93.7 us: ring_gather(): earlier.append(lax.ppermute(earlier[-1], axis, up))]
    dot_general x2, matrix products: 9.58 us -> 59.3 us  [apply_curvature(): project = jnp.dot(train_feats, gathered, preferred_element_type=jnp.float32)]
  transfers between devices with their start and end apart: 8 -> 12, of which waited for: 8 -> 10; matrix products, arithmetic and copies ran while one was open for 0% -> 0% of each run, Pallas kernels for 0% -> 0%
where the time goes in v1:
time: 871 us; the launch traced here: 865 us
  blocking collectives  386 us (44%)
  waiting for transfers between devices  347 us (40%)
  matrix products  88.7 us (10%)
  between operations  20.5 us (2%)
  other arithmetic  13.2 us (2%)
    psum x3, blocking collectives, solver_total(): return lax.psum(value, ('dp', 'fsdp'))  193 us
    psum x2, blocking collectives, apply_curvature(): response = lax.psum(jnp.sum(train_mix * project, axis=1), 'fsdp')  130 us
    ppermute x4, waiting for transfers between devices, ring_gather(): earlier.append(lax.ppermute(earlier[-1], axis, up))  93.7 us
    psum x1, blocking collectives, local(): scores_all = lax.psum(jnp.sum(output_act * head_weight, axis=1), 'fsdp')  62.7 us
    dot_general x2, matrix products, apply_curvature(): project = jnp.dot(train_feats, gathered, preferred_element_type=jnp.float32)  59.3 us
    all_gather x1, waiting for transfers between devices, local(): feats = lax.all_gather(local_rows, 'fsdp', axis=1, tiled=True)  53.5 us
    all_gather x1, waiting for transfers between devices, local(): lax.all_gather(hidden, 'fsdp', axis=1, tiled=True)  49.4 us
    reduce_scatter x1, waiting for transfers between devices, local(): lax.psum_scatter(grad_local.astype(jnp.bfloat16), 'dp', scatter_dimension...  48.5 us
  transfers between devices with their start and end apart: 12, of which 10 were waited for; matrix products, arithmetic and copies ran while one was open for 0% of the time, Pallas kernels for 0%

profile of v1, /device:TPU:1, one launch (start us, length us, event | category | flops | bytes accessed | tf_op | source)
XLA Modules:
  0.0 864.7 jit_solution(5373859666927964667)
XLA Ops:
  7.2 0.8 slice_bitcast_fusion.3
  8.0 0.8 slice_bitcast_fusion.1
  8.7 0.1 fusion.59
  8.8 2.0 gather_fusion
  10.8 0.1 compare_and_fusion
  10.9 0.8 broadcast_select_fusion
  11.7 0.0 all-gather.5.cloned.1.call-start
  11.8 53.5 %all-gather.3.cloned.1.call-done = bf16[272,8192]{1,0:T(8,128)(2,1)} async-done(((bf16[272,256]{1,0:T(8,128)(2,1)}), bf16[272,8192]{1,0:T(8,128)(2,1)}) %all-gather.3.cloned.1.call-update) | async-done | bytes 4456464 | tf_op jit(solution)/shard_map/all_gather | solution.py:48
  65.2 5.5 fusion.37
  70.8 0.0 reduce-scatter.5.cloned.1.call-start
  70.8 49.4 %all-gather.5.cloned.1.call-done = bf16[272,8192]{1,0:T(8,128)(2,1)} async-done(((bf16[272,256]{1,0:T(8,128)(2,1)}), bf16[272,8192]{1,0:T(8,128)(2,1)}) %all-gather.5.cloned.1.call-update) | async-done | bytes 4456464 | tf_op jit(solution)/shard_map/all_gather | solution.py:53
  120.2 5.1 multiply_reduce_fusion.3
  125.4 3.5 convolution_convert_fusion
  128.9 0.0 reduce-scatter.7.cloned.1.call-start
  128.9 62.7 %psum.49 = f32[272]{0:T(512)S(1)} all-reduce(f32[272]{0:T(512)S(1)} %get-tuple-element.24), channel_id=1, replica_groups=mesh['dp'=4,'fsdp'=32] {'fsdp'}, use_global_device_ids=true, to_apply=%region_1.2 | all-reduce | flops 272 | bytes 2176 | tf_op jit(solution)/shard_map/psum | solution.py:58
  191.6 0.1 fusion.65
  191.7 0.1 pad_maximum_fusion.2
  191.7 18.3 %reduce-scatter.5.cloned.1.call-done = bf16[272,256]{1,0:T(8,128)(2,1)} async-done(((bf16[272,8192]{1,0:T(8,128)(2,1)}), bf16[272,256]{1,0:T(8,128)(2,1)}) %reduce-scatter.5.cloned.1.call-update) | async-done | bytes 139280 | tf_op jit(solution)/shard_map/reduce_scatter | solution.py:63
  210.1 1.0 convert_multiply_fusion.5
  211.0 4.3 convolution_convert_fusion.3
  215.4 0.0 reduce-scatter.9.cloned.1.call-start
  215.4 48.5 %reduce-scatter.7.cloned.1.call-done = bf16[2048,256]{1,0:T(8,128)(2,1)} async-done(((bf16[8192,256]{1,0:T(8,128)(2,1)}), bf16[2048,256]{1,0:T(8,128)(2,1)}) %reduce-scatter.7.cloned.1.call-update) | async-done | bytes 1048592 | tf_op jit(solution)/shard_map/reduce_scatter | solution.py:75
  264.0 2.7 collective-permute-start.2
  266.6 22.8 %collective-permute-done = bf16[2048,256]{1,0:T(8,128)(2,1)S(1)} collective-permute-done((bf16[2048,256]{1,0:T(8,128)(2,1)}, bf16[2048,256]{1,0:T(8,128)(2,1)S(1)}, u32[]{:S(2)}, u32[]{:S(2)}) %collective-permute-start) | collective-permute-done | bytes 1048608 | tf_op jit(solution)/shard_map/ppermute | solution.py:15
  289.4 0.3 collective-permute-start.1
  289.8 24.4 %collective-permute-done.1 = bf16[2048,256]{1,0:T(8,128)(2,1)} collective-permute-done((bf16[2048,256]{1,0:T(8,128)(2,1)S(1)}, bf16[2048,256]{1,0:T(8,128)(2,1)}, u32[]{:S(2)}, u32[]{:S(2)}) %collective-permute-start.1) | collective-permute-done | bytes 1048608 | tf_op jit(solution)/shard_map/ppermute | solution.py:15
  314.2 23.2 %fusion.39 = f32[256]{0:T(256)S(1)} fusion(s32[]{:T(128)S(6)} %select_n.36, bf16[2048,256]{1,0:T(8,128)(2,1)} %collective-permute-done.1, bf16[2048,256]{1,0:T(8,128)(2,1)S(1)} %collective-permute-done, bf16[2048,256]{1,0:T(8,128)(2,1)} %reduce-scatter.7.cloned.1.call-done, bf16[2048,256]{1,0:T(8,128)(2,1)S(1)} %collective-permute-done.2, ...), kind=kOutput, calls=%fused_computation.62 | convolution fusion | flops 1107427072 | bytes 8651780 | tf_op jit(solution)/shard_map/dot_general | solution.py:84
  337.4 65.0 %psum.51 = f32[256]{0:T(256)S(1)} all-reduce(f32[256]{0:T(256)S(1)} %fusion.39), channel_id=1, replica_groups=mesh['dp'=4,'fsdp'=32] {'fsdp'}, use_global_device_ids=true, to_apply=%region_7.9 | all-reduce | flops 256 | bytes 2048 | tf_op jit(solution)/shard_map/psum | solution.py:85
  402.4 5.5 convolution_convert_fusion.2
  408.0 0.0 reduce-scatter.11.cloned.1.call-start
  408.0 43.1 %reduce-scatter.9.cloned.1.call-done = bf16[2048,256]{1,0:T(8,128)(2,1)} async-done(((bf16[8192,256]{1,0:T(8,128)(2,1)}), bf16[2048,256]{1,0:T(8,128)(2,1)}) %reduce-scatter.9.cloned.1.call-update) | async-done | bytes 1048592 | tf_op jit(solution)/shard_map/reduce_scatter | solution.py:94
  451.1 2.5 fusion.24
  453.6 64.6 %all-reduce = (f32[]{:T(128)}, f32[]{:T(128)}) all-reduce(f32[]{:T(128)} %get-tuple-element.4, f32[]{:T(128)} %get-tuple-element.3), channel_id=1, replica_groups=mesh['dp'=4,'fsdp'=32] {'dp','fsdp'}, use_global_device_ids=true, to_apply=%region_5.6 | all-reduce | flops 2 | bytes 16 | tf_op jit(solution)/shard_map/psum | solution.py:31
  520.2 2.4 multiply_reduce_fusion.2
  522.6 64.1 %psum.53 = f32[]{:T(128)} all-reduce(f32[]{:T(128)} %multiply_reduce_fusion.2), channel_id=1, replica_groups=mesh['dp'=4,'fsdp'=32] {'dp','fsdp'}, use_global_device_ids=true, to_apply=%region_12.14 | all-reduce | flops 1 | bytes 8 | tf_op jit(solution)/shard_map/psum | solution.py:31
  588.1 1.3 multiply_reduce_fusion
  589.4 2.7 collective-permute-start.5
  592.1 22.4 %collective-permute-done.3 = bf16[2048,256]{1,0:T(8,128)(2,1)S(1)} collective-permute-done((bf16[2048,256]{1,0:T(8,128)(2,1)S(1)}, bf16[2048,256]{1,0:T(8,128)(2,1)S(1)}, u32[]{:S(2)}, u32[]{:S(2)}) %collective-permute-start.3) | collective-permute-done | bytes 1048608 | tf_op jit(solution)/shard_map/ppermute | solution.py:15
  614.5 0.2 collective-permute-start.4
  614.7 24.1 %collective-permute-done.4 = bf16[2048,256]{1,0:T(8,128)(2,1)S(1)} collective-permute-done((bf16[2048,256]{1,0:T(8,128)(2,1)S(1)}, bf16[2048,256]{1,0:T(8,128)(2,1)S(1)}, u32[]{:S(2)}, u32[]{:S(2)}) %collective-permute-start.4) | collective-permute-done | bytes 1048608 | tf_op jit(solution)/shard_map/ppermute | solution.py:15
  638.8 36.1 %fusion.44 = f32[256]{0:T(256)S(1)} fusion(s32[]{:T(128)S(6)} %select_n.36, bf16[2048,256]{1,0:T(8,128)(2,1)S(1)} %collective-permute-done.4, bf16[2048,256]{1,0:T(8,128)(2,1)S(1)} %collective-permute-done.3, bf16[2048,256]{1,0:T(8,128)(2,1)S(1)} %get-tuple-element.13, bf16[2048,256]{1,0:T(8,128)(2,1)S(1)} %collective-permute-done.5, ...), kind=kOutput, calls=%fused_computation.63 | convolution fusion | flops 1107427072 | bytes 8651780 | tf_op jit(solution)/shard_map/dot_general | solution.py:84
  674.8 64.8 %psum.54 = f32[256]{0:T(256)S(1)} all-reduce(f32[256]{0:T(256)S(1)} %fusion.44), channel_id=1, replica_groups=mesh['dp'=4,'fsdp'=32] {'fsdp'}, use_global_device_ids=true, to_apply=%region_14.16 | all-reduce | flops 256 | bytes 2048 | tf_op jit(solution)/shard_map/psum | solution.py:85
  739.7 5.5 convolution_convert_fusion.1
  745.9 40.3 %reduce-scatter.11.cloned.1.call-done = bf16[2048,256]{1,0:T(8,128)(2,1)} async-done(((bf16[8192,256]{1,0:T(8,128)(2,1)}), bf16[2048,256]{1,0:T(8,128)(2,1)}) %reduce-scatter.11.cloned.1.call-update) | async-done | bytes 1048592 | tf_op jit(solution)/shard_map/reduce_scatter | solution.py:107
  786.2 2.4 multiply_reduce_fusion.1
  789.2 64.5 %psum.55 = f32[]{:T(128)} all-reduce(f32[]{:T(128)S(6)} %add.92), channel_id=1, replica_groups=mesh['dp'=4,'fsdp'=32] {'dp','fsdp'}, use_global_device_ids=true, to_apply=%region_18.20 | all-reduce | flops 1 | bytes 8 | tf_op jit(solution)/shard_map/psum | solution.py:31
  855.0 0.5 add_multiply_fusion
  855.6 2.1 fusion.25
  (35 shorter events, 0.3 us)
Async XLA Ops:
  7.2 1.7 copy-start
  7.2 58.0 %all-gather.3.cloned.1.call-start = ((), (), s32[]{:S(2)}) async-start(), calls=%async_computation.4 | async-start | bytes 4595712 | tf_op jit(solution)/shard_map/all_gather | solution.py:48
  11.7 108.5 %copy-start.6 = (f32[256]{0:T(256)S(1)}, f32[256]{0:T(256)}, u32[]{:S(2)}) copy-start(f32[256]{0:T(256)} %param.17) | copy-start | bytes 3076
  11.7 108.5 %all-gather.5.cloned.1.call-start = ((), (), s32[]{:S(2)}) async-start(), calls=%async_computation.5 | async-start | bytes 4595712 | tf_op jit(solution)/shard_map/all_gather | solution.py:53
  70.8 139.3 %reduce-scatter.5.cloned.1.call-start = ((), (), s32[]{:S(2)}) async-start(), calls=%async_computation.6 | async-start | bytes 4595712 | tf_op jit(solution)/shard_map/reduce_scatter | solution.py:63
  120.2 5.1 copy-start.3
  128.8 62.8 %copy-start.8 = (s32[8]{0:T(128)S(1)}, s32[8]{0:T(128)}, u32[]{:S(2)}) copy-start(s32[8]{0:T(128)} %param.14) | copy-start | bytes 100
  128.8 81.3 %copy-start.4 = (bf16[272,256]{1,0:T(8,128)(2,1)S(1)}, bf16[272,256]{1,0:T(8,128)(2,1)}, u32[]{:S(2)}) copy-start(bf16[272,256]{1,0:T(8,128)(2,1)} %fusion.37) | copy-start | bytes 417796
  128.9 135.1 %reduce-scatter.7.cloned.1.call-start = ((), (), s32[]{:S(2)}) async-start(), calls=%async_computation.7 | async-start | bytes 5242880 | tf_op jit(solution)/shard_map/reduce_scatter | solution.py:75
  211.0 191.4 %copy-start.5 = (f32[272,256]{1,0:T(8,128)}, f32[272,256]{1,0:T(8,128)S(1)}, u32[]{:S(2)}) copy-start(f32[272,256]{1,0:T(8,128)S(1)} %convert_multiply_fusion.5) | copy-start | bytes 835588
  215.4 235.7 %reduce-scatter.9.cloned.1.call-start = ((), (), s32[]{:S(2)}) async-start(), calls=%async_computation.8 | async-start | bytes 5242880 | tf_op jit(solution)/shard_map/reduce_scatter | solution.py:94
  263.9 25.5 %collective-permute-start = (bf16[2048,256]{1,0:T(8,128)(2,1)}, bf16[2048,256]{1,0:T(8,128)(2,1)S(1)}, u32[]{:S(2)}, u32[]{:S(2)}) collective-permute-start(bf16[2048,256]{1,0:T(8,128)(2,1)} %reduce-scatter.7.cloned.1.call-done), channel_id=1, source_target_pairs={{0,32},{32,64},{64,96},{96,0},{1,33},{33,65},{65,97},{97,1},{2,34}... | collective-permute-start | bytes 3145736 | tf_op jit(solution)/shard_map/ppermute | solution.py:15
  264.0 25.8 %collective-permute-start.2 = (bf16[2048,256]{1,0:T(8,128)(2,1)}, bf16[2048,256]{1,0:T(8,128)(2,1)S(1)}, u32[]{:S(2)}, u32[]{:S(2)}) collective-permute-start(bf16[2048,256]{1,0:T(8,128)(2,1)} %reduce-scatter.7.cloned.1.call-done), channel_id=1, source_target_pairs={{0,96},{32,0},{64,32},{96,64},{1,97},{33,1},{65,33},{97,65},{2,98}... | collective-permute-start | bytes 3145736 | tf_op jit(solution)/shard_map/ppermute | solution.py:17
  289.4 24.7 %collective-permute-start.1 = (bf16[2048,256]{1,0:T(8,128)(2,1)S(1)}, bf16[2048,256]{1,0:T(8,128)(2,1)}, u32[]{:S(2)}, u32[]{:S(2)}) collective-permute-start(bf16[2048,256]{1,0:T(8,128)(2,1)S(1)} %collective-permute-done), channel_id=1, source_target_pairs={{0,32},{32,64},{64,96},{96,0},{1,33},{33,65},{65,97},{97,1},{2,34}... | collective-permute-start | bytes 3145736 | tf_op jit(solution)/shard_map/ppermute | solution.py:15
  289.7 112.6 %copy-start.7 = (s32[128]{0:T(128)S(1)}, s32[128]{0:T(128)}, u32[]{:S(2)}) copy-start(s32[128]{0:T(128)} %param.12) | copy-start | bytes 1540
  407.9 43.2 %copy-start.1 = (bf16[2048,256]{1,0:T(8,128)(2,1)S(1)}, bf16[2048,256]{1,0:T(8,128)(2,1)}, u32[]{:S(2)}) copy-start(bf16[2048,256]{1,0:T(8,128)(2,1)} %reduce-scatter.7.cloned.1.call-done) | copy-start | bytes 3145732
  408.0 378.2 %reduce-scatter.11.cloned.1.call-start = ((), (), s32[]{:S(2)}) async-start(), calls=%async_computation.9 | async-start | bytes 5242880 | tf_op jit(solution)/shard_map/reduce_scatter | solution.py:107
  451.1 137.0 %copy-start.2 = (bf16[2048,256]{1,0:T(8,128)(2,1)S(1)}, bf16[2048,256]{1,0:T(8,128)(2,1)}, u32[]{:S(2)}) copy-start(bf16[2048,256]{1,0:T(8,128)(2,1)} %reduce-scatter.9.cloned.1.call-done) | copy-start | bytes 3145732
  589.4 25.1 %collective-permute-start.3 = (bf16[2048,256]{1,0:T(8,128)(2,1)S(1)}, bf16[2048,256]{1,0:T(8,128)(2,1)S(1)}, u32[]{:S(2)}, u32[]{:S(2)}) collective-permute-start(bf16[2048,256]{1,0:T(8,128)(2,1)S(1)} %get-tuple-element.13), channel_id=1, source_target_pairs={{0,32},{32,64},{64,96},{96,0},{1,33},{33,65},{65,97},{97,1},{2,34}... | collective-permute-start | bytes 3145736 | tf_op jit(solution)/shard_map/ppermute | solution.py:15
  589.4 25.2 %collective-permute-start.5 = (bf16[2048,256]{1,0:T(8,128)(2,1)S(1)}, bf16[2048,256]{1,0:T(8,128)(2,1)S(1)}, u32[]{:S(2)}, u32[]{:S(2)}) collective-permute-start(bf16[2048,256]{1,0:T(8,128)(2,1)S(1)} %get-tuple-element.13), channel_id=1, source_target_pairs={{0,96},{32,0},{64,32},{96,64},{1,97},{33,1},{65,33},{97,65},{2,98}... | collective-permute-start | bytes 3145736 | tf_op jit(solution)/shard_map/ppermute | solution.py:17
  614.5 24.3 %collective-permute-start.4 = (bf16[2048,256]{1,0:T(8,128)(2,1)S(1)}, bf16[2048,256]{1,0:T(8,128)(2,1)S(1)}, u32[]{:S(2)}, u32[]{:S(2)}) collective-permute-start(bf16[2048,256]{1,0:T(8,128)(2,1)S(1)} %collective-permute-done.3), channel_id=1, source_target_pairs={{0,32},{32,64},{64,96},{96,0},{1,33},{33,65},{65,97},{97,1},{2,34}... | collective-permute-start | bytes 3145736 | tf_op jit(solution)/shard_map/ppermute | solution.py:15
Sparse Core Ops, SparseCore 0:
  11.8 53.3 all-gather.2
  70.9 49.2 all-gather.4
  129.0 81.0 reduce-scatter.4
  215.5 48.3 reduce-scatter.6
  408.1 42.9 reduce-scatter.8
  745.4 40.7 reduce-scatter.10
